TPU v7x, 32 devices: a whole 2x2x4 slice. The times are simulated.
32 devices in a mesh: groups: 2 (over x), member: 2 (over core), tile: 8 (over z, y).
Axes of the slice: x: 2, y: 2, z: 4, core: 2. Of those that a mesh axis runs over, the one named last changes fastest.
Arguments:
- state: float32 [8, 4, 4, 512, 256], P(('groups', 'member'), None, None, 'tile'), parts along dimension 0, may hold values from -6 to 6
- perturbation: float32 [8, 4, 4, 512, 256], P(('groups', 'member'), None, None, 'tile'), parts along dimension 0, may hold values from -2 to 2
- ancestors: int32 [8], P('groups'), parts along dimension 0, may hold values from 0 to 3, as said below
Outputs:
- evolved: float32 [8, 4, 4, 512, 256], P(('groups', 'member'), None, None, 'tile'), parts along dimension 0
- observable: float32 [8], P(('groups', 'member')), parts along dimension 0
There are 2 independent parts, one for each index of `groups`. A program takes and returns all parts, laid end to end along the dimension named above; each array names one. Nothing has to cross between parts.
Inputs may be any that keep to these rules, and one draw needn't show every extreme that they name: `ancestors`: surviving slots name themselves; every other slot names a surviving slot; at least two slots survive and at least one does not.
All inputs are finite; a program needn't handle non-finite values.
Results may differ from a plain program's by a relative error of at most 0.00002.
Values sent between devices are 32-bit elements; how exact they have to be, the bound alone decides.
A program may use at most 64 MiB of HBM per device.

v0:
```python
import jax
import jax.numpy as jnp
from jax import lax
from jax.sharding import PartitionSpec as P

STEPS_EACH = 2


TIME_STEP = 0.15
DIFFUSION = 0.2
MIXING = 0.1
CORIOLIS = 0.5
BUOYANCY_GAIN = 0.3
STRATIFICATION = 0.3
SATURATION = 0.5
LATENT = 0.5


def extended(cells, sides, width):
    for axis, dim in sides:
        count = lax.axis_size(axis)
        ends = count - 1
        head = lax.slice_in_dim(cells, 0, width, axis=dim)
        tail = lax.slice_in_dim(cells, cells.shape[dim] - width, cells.shape[dim], axis=dim)
        cells = jnp.concatenate(
            [
                lax.ppermute(tail, axis, [(i, (i + 1) % count) for i in range(ends)]),
                cells,
                lax.ppermute(head, axis, [((i + 1) % count, i) for i in range(ends)]),
            ],
            axis=dim,
        )
    return cells


def advance_core(padded):
    centre = padded[:, :, :, 2:-2, :]
    north_one = padded[:, :, :, 3:-1, :]
    south_one = padded[:, :, :, 1:-3, :]
    north_two = padded[:, :, :, 4:, :]
    south_two = padded[:, :, :, :-4, :]
    east_one = jnp.roll(centre, -1, axis=4)
    west_one = jnp.roll(centre, 1, axis=4)
    east_two = jnp.roll(centre, -2, axis=4)
    west_two = jnp.roll(centre, 2, axis=4)
    slope_y = (8.0 * (north_one - south_one) - (north_two - south_two)) / 12.0
    slope_x = (8.0 * (east_one - west_one) - (east_two - west_two)) / 12.0
    laplace = north_one + south_one + east_one + west_one - 4.0 * centre
    upper = jnp.concatenate([centre[:, :, 1:], centre[:, :, -1:]], axis=2)
    lower = jnp.concatenate([centre[:, :, :1], centre[:, :, :-1]], axis=2)
    vertical = upper + lower - 2.0 * centre
    east_wind = centre[:, 0:1]
    north_wind = centre[:, 1:2]
    buoyancy = centre[:, 2:3]
    tendency = (
        -(east_wind * slope_x + north_wind * slope_y) + DIFFUSION * laplace + MIXING * vertical
    )
    forcing = jnp.concatenate(
        [
            CORIOLIS * north_wind,
            -CORIOLIS * east_wind + BUOYANCY_GAIN * buoyancy,
            -STRATIFICATION * north_wind,
            jnp.zeros_like(north_wind),
        ],
        axis=1,
    )
    updated = centre + TIME_STEP * (tendency + forcing)
    buoyancy_new = updated[:, 2:3]
    moisture = updated[:, 3:4]
    excess = jnp.maximum(moisture - SATURATION * jnp.exp(0.1 * buoyancy_new), 0.0)
    return jnp.concatenate(
        [updated[:, 0:2], buoyancy_new + LATENT * excess, moisture - excess], axis=1
    )


def advance_all(fields):
    for number in range(STEPS_EACH):
        padded = extended(fields, (("tile", 3),), 2)
        fields = advance_core(padded)
    return fields


def body(state, perturbation, ancestors):
    count_dev = state.shape[0]
    owner = lax.axis_index("member")
    fields = advance_all(state)
    member_count = lax.axis_size("member")
    slot_source = ancestors - owner * count_dev
    mine = (slot_source >= 0) & (slot_source < count_dev)
    outgoing = jnp.take(fields, jnp.clip(slot_source, 0, count_dev - 1), axis=0)
    outgoing = jnp.where(mine[:, None, None, None, None], outgoing, 0.0)
    incoming = lax.all_to_all(outgoing, "member", split_axis=0, concat_axis=0, tiled=True)
    cloned = jnp.sum(incoming.reshape((member_count, count_dev) + fields.shape[1:]), axis=0)
    fields = advance_all(cloned + perturbation)
    rows_here = fields.shape[3]
    total_rows = rows_here * lax.axis_size("tile")
    latitude = (lax.axis_index("tile") * rows_here + jnp.arange(rows_here, dtype=jnp.int32)).astype(
        jnp.float32
    )
    weight = 1.0 + 2.0 * latitude / (total_rows - 1)
    buoyancy = fields[:, 2]
    partial_total = jnp.sum(weight[:, None] * buoyancy * buoyancy, axis=(1, 2, 3))
    total = lax.psum(partial_total, "tile")
    observable = total / (fields.shape[2] * total_rows * fields.shape[4])
    return (fields, observable)


def solution(mesh):
    return jax.shard_map(
        body,
        mesh=mesh,
        in_specs=(
            P(("groups", "member"), None, None, "tile", None),
            P(("groups", "member"), None, None, "tile", None),
            P("groups"),
        ),
        out_specs=(P(("groups", "member"), None, None, "tile", None), P(("groups", "member"))),
        check_vma=False,
    )
```

profile of v0, /device:TPU:0, one launch (start us, length us, event | category | flops | bytes accessed | tf_op | source)
XLA Modules:
  0.0 146.0 jit_solution(2485772114257159055)
XLA Ops:
  3.0 5.7 %collective-permute-start.1 = (f32[2,4,4,2,256]{4,3,2,1,0:T(2,128)S(1)}, f32[2,4,4,2,256]{4,3,2,1,0:T(2,128)S(1)}, u32[]{:S(2)}, u32[]{:S(2)}) collective-permute-start(f32[2,4,4,2,256]{4,3,2,1,0:T(2,128)S(1)} %get-tuple-element.95), channel_id=1, source_target_pairs={{0,1},{1,2},{2,3},{3,4},{4,5},{5,6},{6,7},{8,9},{9,10},{10,11},{11... | collective-permute-start | bytes 196616 | tf_op jit(solution)/shard_map/ppermute | solution.py:27
  8.7 2.9 %multiply_bitcast_fusion.7 = (f32[2,4,64,256]{3,2,1,0:T(8,128)}, f32[2,1,4,64,256]{4,3,2,1,0:T(8,128)}, f32[2,1,4,64,256]{4,3,2,1,0:T(8,128)}, f32[2,4,64,256]{3,2,1,0:T(8,128)}, f32[2,1,4,64,256]{4,3,2,1,0:T(8,128)}) fusion(f32[2,4,4,64,256]{4,3,2,1,0:T(8,128)} %param.3), kind=kLoop, calls=%fused_computation.124 | loop fusion | flops 917504 | bytes 4194304 | tf_op jit(solution)/shard_map/mul | solution.py:56
  13.2 2.8 %fusion.84 = (f32[2,4,4,64,255]{4,3,2,1,0:T(8,128)}, f32[2,4,4,64,255]{4,3,2,1,0:T(8,128)}) fusion(f32[2,4,4,64,256]{4,3,2,1,0:T(8,128)S(1)} %copy-done), kind=kLoop, calls=%fused_computation.162 | loop fusion | bytes 8355840 | tf_op jit(solution)/shard_map/jit(_roll_static)/slice | solution.py:42
  16.0 2.8 %fusion.89 = (f32[2,4,4,64,254]{4,3,2,1,0:T(8,128)}, f32[2,4,4,64,254]{4,3,2,1,0:T(8,128)}) fusion(f32[2,4,4,64,256]{4,3,2,1,0:T(8,128)S(1)} %copy-done), kind=kLoop, calls=%fused_computation.167 | loop fusion | bytes 8323072 | tf_op jit(solution)/shard_map/jit(_roll_static)/slice | solution.py:45
  18.8 2.1 %fusion.87 = (f32[2,4,3,64,256]{4,3,2,1,0:T(8,128)}, f32[2,4,3,64,256]{4,3,2,1,0:T(8,128)}) fusion(f32[2,4,4,64,256]{4,3,2,1,0:T(8,128)S(1)} %copy-done), kind=kLoop, calls=%fused_computation.165 | loop fusion | bytes 6291456 | tf_op jit(solution)/shard_map/slice | solution.py:50
  20.9 1.7 %fusion.85 = (f32[2,4,4,64,1]{4,3,2,1,0:T(8,128)}, f32[2,4,4,64,1]{4,3,2,1,0:T(8,128)}) fusion(f32[2,4,4,64,256]{4,3,2,1,0:T(8,128)S(1)} %copy-done), kind=kLoop, calls=%fused_computation.163 | loop fusion | bytes 32768 | tf_op jit(solution)/shard_map/jit(_roll_static)/slice | solution.py:42
  22.5 1.7 %fusion.88 = (f32[2,4,4,64,2]{4,3,2,1,0:T(8,128)}, f32[2,4,4,64,2]{4,3,2,1,0:T(8,128)}) fusion(f32[2,4,4,64,256]{4,3,2,1,0:T(8,128)S(1)} %copy-done), kind=kLoop, calls=%fused_computation.166 | loop fusion | bytes 65536 | tf_op jit(solution)/shard_map/jit(_roll_static)/slice | solution.py:45
  25.9 9.7 %fusion.5 = f32[2,4,4,64,256]{4,3,2,1,0:T(8,128)S(1)} fusion(f32[2,4,4,64,256]{4,3,2,1,0:T(8,128)S(1)} %copy-done, f32[2,1,4,64,256]{4,3,2,1,0:T(8,128)S(1)} %broadcast.118, f32[2,4,4,2,256]{4,3,2,1,0:T(2,128)S(1)} %collective-permute-done.1, f32[2,4,4,66,256]{4,3,2,1,0:T(8,128)} %constant_dynamic-update-slice_fusion, ...), kind=kLoop, calls=%fused_computation.21 | loop fusion | flops 19922944 | bytes 24182784 | tf_op jit(solution)/shard_map/add | solution.py:67
  39.7 1.7 %fusion.78 = (f32[2,4,4,64,1]{4,3,2,1,0:T(8,128)}, f32[2,4,4,64,1]{4,3,2,1,0:T(8,128)}) fusion(f32[2,4,4,64,256]{4,3,2,1,0:T(8,128)S(1)} %pad_maximum_fusion.11), kind=kLoop, calls=%fused_computation.156 | loop fusion | bytes 32768 | tf_op jit(solution)/shard_map/jit(_roll_static)/slice | solution.py:42
  41.3 1.7 %fusion.81 = (f32[2,4,4,64,2]{4,3,2,1,0:T(8,128)}, f32[2,4,4,64,2]{4,3,2,1,0:T(8,128)}) fusion(f32[2,4,4,64,256]{4,3,2,1,0:T(8,128)S(1)} %pad_maximum_fusion.11), kind=kLoop, calls=%fused_computation.159 | loop fusion | bytes 65536 | tf_op jit(solution)/shard_map/jit(_roll_static)/slice | solution.py:45
  44.3 5.4 %collective-permute-start.3 = (f32[2,4,4,2,256]{4,3,2,1,0:T(2,128)S(1)}, f32[2,4,4,2,256]{4,3,2,1,0:T(2,128)S(1)}, u32[]{:S(2)}, u32[]{:S(2)}) collective-permute-start(f32[2,4,4,2,256]{4,3,2,1,0:T(2,128)S(1)} %get-tuple-element.76), channel_id=1, source_target_pairs={{0,1},{1,2},{2,3},{3,4},{4,5},{5,6},{6,7},{8,9},{9,10},{10,11},{11... | collective-permute-start | bytes 196616 | tf_op jit(solution)/shard_map/ppermute | solution.py:27
  52.1 5.7 %fusion.8 = f32[2,4,4,64,256]{4,3,2,1,0:T(8,128)S(1)} fusion(f32[2,1,4,64,256]{4,3,2,1,0:T(8,128)S(1)} %broadcast.118, f32[2,4,4,66,256]{4,3,2,1,0:T(8,128)S(1)} %get-tuple-element.74, f32[2,4,4,66,256]{4,3,2,1,0:T(8,128)S(1)} %get-tuple-element.73, f32[2,4,4,64,2]{4,3,2,1,0:T(8,128)} %get-tuple-element.70, f32[2,4,4,64,254]{4,3,2,1,0:T(8,128)S(1)} %get-tuple-element.72, ...), kind=kLoop, calls=%fused_computation.24 | loop fusion | flops 19922944 | bytes 28311552 | tf_op jit(solution)/shard_map/add | solution.py:67
  58.4 2.8 %gather_fusion = f32[4,4,4,64,256]{4,3,2,1,0:T(8,128)} fusion(f32[2,4,4,64,256]{4,3,2,1,0:T(8,128)S(1)} %pad_maximum_fusion.14, s32[1024]{0:T(1024)S(1)} %pad_clamp_fusion), kind=kCustom, calls=%fused_computation | custom fusion | bytes 8388624 | tf_op jit(solution)/shard_map/jit(_take)/gather | solution.py:90
  61.2 2.7 %select_select_fusion = f32[4,4,4,64,256]{4,3,2,1,0:T(8,128)S(1)} fusion(f32[4,4,4,64,256]{4,3,2,1,0:T(8,128)} %gather_fusion, pred[4]{0:T(512)(128)(4,1)S(1)} %get-tuple-element.6, pred[4]{0:T(512)(128)(4,1)S(1)} %get-tuple-element.96), kind=kLoop, calls=%fused_computation.5 | loop fusion | flops 2097152 | bytes 8388616 | tf_op jit(solution)/shard_map/jit(_where)/select_n | solution.py:91
  63.9 8.2 %all_to_all.5 = f32[4,4,4,64,256]{4,3,2,1,0:T(8,128)} all-to-all(f32[4,4,4,64,256]{4,3,2,1,0:T(8,128)S(1)} %select_select_fusion), channel_id=1, replica_groups=mesh['groups'=2,'member'=2,'tile'=8] {'member'}, dimensions={0} | all-to-all | bytes 8388608 | tf_op jit(solution)/shard_map/all_to_all | solution.py:92
  72.1 2.7 %reduce_sum.18 = f32[2,4,4,64,256]{4,3,2,1,0:T(8,128)S(1)} reduce(f32[2,2,4,4,64,256]{5,4,3,2,1,0:T(8,128)} %bitcast.19, f32[]{:T(128)} %constant.68.clone.1), dimensions={0}, to_apply=%region_0.1 | reduce | flops 524288 | bytes 6291460 | tf_op jit(solution)/shard_map/reduce_sum | solution.py:93
  74.9 1.9 %add.184 = f32[2,4,4,64,256]{4,3,2,1,0:T(8,128)S(1)} add(f32[2,4,4,64,256]{4,3,2,1,0:T(8,128)S(1)} %reduce_sum.18, f32[2,4,4,64,256]{4,3,2,1,0:T(8,128)} %param.4) | non-fusion elementwise | flops 524288 | bytes 6291456 | tf_op jit(solution)/shard_map/add | solution.py:94
  82.3 5.4 %collective-permute-start.5 = (f32[2,4,4,2,256]{4,3,2,1,0:T(2,128)S(1)}, f32[2,4,4,2,256]{4,3,2,1,0:T(2,128)S(1)}, u32[]{:S(2)}, u32[]{:S(2)}) collective-permute-start(f32[2,4,4,2,256]{4,3,2,1,0:T(2,128)S(1)} %get-tuple-element.51), channel_id=1, source_target_pairs={{0,1},{1,2},{2,3},{3,4},{4,5},{5,6},{6,7},{8,9},{9,10},{10,11},{11... | collective-permute-start | bytes 196616 | tf_op jit(solution)/shard_map/ppermute | solution.py:27
  88.6 1.8 %collective-permute-done.5 = f32[2,4,4,2,256]{4,3,2,1,0:T(2,128)S(1)} collective-permute-done((f32[2,4,4,2,256]{4,3,2,1,0:T(2,128)S(1)}, f32[2,4,4,2,256]{4,3,2,1,0:T(2,128)S(1)}, u32[]{:S(2)}, u32[]{:S(2)}) %collective-permute-start.5) | collective-permute-done | bytes 65568 | tf_op jit(solution)/shard_map/ppermute | solution.py:27
  91.1 5.9 %fusion.11 = f32[2,4,4,64,256]{4,3,2,1,0:T(8,128)S(1)} fusion(f32[2,4,4,64,256]{4,3,2,1,0:T(8,128)S(1)} %add.184, f32[2,1,4,64,256]{4,3,2,1,0:T(8,128)S(1)} %broadcast.118, f32[2,4,4,2,256]{4,3,2,1,0:T(2,128)} %copy-done.2, f32[2,4,4,2,256]{4,3,2,1,0:T(2,128)} %copy-done.1, f32[2,4,4,64,2]{4,3,2,1,0:T(8,128)S(1)} %get-tuple-element.47, ...), kind=kLoop, calls=%fused_computation.27 | loop fusion | flops 20971520 | bytes 20054016 | tf_op jit(solution)/shard_map/add | solution.py:67
  102.6 1.7 %fusion.67 = (f32[2,4,4,64,2]{4,3,2,1,0:T(8,128)}, f32[2,4,4,64,2]{4,3,2,1,0:T(8,128)}) fusion(f32[2,4,4,64,256]{4,3,2,1,0:T(8,128)S(1)} %pad_maximum_fusion.17), kind=kLoop, calls=%fused_computation.145 | loop fusion | bytes 65536 | tf_op jit(solution)/shard_map/jit(_roll_static)/slice | solution.py:45
  105.6 5.0 %collective-permute-start.7 = (f32[2,4,4,2,256]{4,3,2,1,0:T(2,128)S(1)}, f32[2,4,4,2,256]{4,3,2,1,0:T(2,128)S(1)}, u32[]{:S(2)}, u32[]{:S(2)}) collective-permute-start(f32[2,4,4,2,256]{4,3,2,1,0:T(2,128)S(1)} %get-tuple-element.32), channel_id=1, source_target_pairs={{0,1},{1,2},{2,3},{3,4},{4,5},{5,6},{6,7},{8,9},{9,10},{10,11},{11... | collective-permute-start | bytes 196616 | tf_op jit(solution)/shard_map/ppermute | solution.py:27
  113.3 5.7 %fusion.14 = f32[2,4,4,64,256]{4,3,2,1,0:T(8,128)S(1)} fusion(f32[2,1,4,64,256]{4,3,2,1,0:T(8,128)S(1)} %broadcast.118, f32[2,4,4,66,256]{4,3,2,1,0:T(8,128)S(1)} %get-tuple-element.30, f32[2,4,4,66,256]{4,3,2,1,0:T(8,128)S(1)} %get-tuple-element.29, f32[2,4,4,64,2]{4,3,2,1,0:T(8,128)} %get-tuple-element.26, f32[2,4,4,64,254]{4,3,2,1,0:T(8,128)S(1)} %get-tuple-element.28, ...), kind=kLoop, calls=%fused_computation.30 | loop fusion | flops 19922944 | bytes 28311552 | tf_op jit(solution)/shard_map/add | solution.py:67
  119.6 24.4 %psum.7 = f32[2]{0:T(128)S(1)} all-reduce(f32[2]{0:T(128)S(1)} %get-tuple-element.2), channel_id=1, replica_groups=mesh['groups'=2,'member'=2,'tile'=8] {'tile'}, use_global_device_ids=true, to_apply=%region_2.3 | all-reduce | flops 2 | bytes 16 | tf_op jit(solution)/shard_map/psum | solution.py:103
  (62 shorter events, 32.9 us)
Async XLA Ops:
  1.7 23.5 %collective-permute-start = (f32[2,4,4,2,256]{4,3,2,1,0:T(2,128)S(1)}, f32[2,4,4,2,256]{4,3,2,1,0:T(2,128)S(1)}, u32[]{:S(2)}, u32[]{:S(2)}) collective-permute-start(f32[2,4,4,2,256]{4,3,2,1,0:T(2,128)S(1)} %get-tuple-element.94), channel_id=1, source_target_pairs={{1,0},{2,1},{3,2},{4,3},{5,4},{6,5},{7,6},{9,8},{10,9},{11,10},{12... | collective-permute-start | bytes 196616 | tf_op jit(solution)/shard_map/ppermute | solution.py:29
  3.0 8.6 %copy-start = (f32[2,4,4,64,256]{4,3,2,1,0:T(8,128)S(1)}, f32[2,4,4,64,256]{4,3,2,1,0:T(8,128)}, u32[]{:S(2)}) copy-start(f32[2,4,4,64,256]{4,3,2,1,0:T(8,128)} %param.3) | copy-start | bytes 6291460
  3.0 22.8 %collective-permute-start.1 = (f32[2,4,4,2,256]{4,3,2,1,0:T(2,128)S(1)}, f32[2,4,4,2,256]{4,3,2,1,0:T(2,128)S(1)}, u32[]{:S(2)}, u32[]{:S(2)}) collective-permute-start(f32[2,4,4,2,256]{4,3,2,1,0:T(2,128)S(1)} %get-tuple-element.95), channel_id=1, source_target_pairs={{0,1},{1,2},{2,3},{3,4},{4,5},{5,6},{6,7},{8,9},{9,10},{10,11},{11... | collective-permute-start | bytes 196616 | tf_op jit(solution)/shard_map/ppermute | solution.py:27
  24.2 0.9 copy-start.3
  43.0 7.8 %collective-permute-start.2 = (f32[2,4,4,2,256]{4,3,2,1,0:T(2,128)S(1)}, f32[2,4,4,2,256]{4,3,2,1,0:T(2,128)S(1)}, u32[]{:S(2)}, u32[]{:S(2)}) collective-permute-start(f32[2,4,4,2,256]{4,3,2,1,0:T(2,128)S(1)} %get-tuple-element.75), channel_id=1, source_target_pairs={{1,0},{2,1},{3,2},{4,3},{5,4},{6,5},{7,6},{9,8},{10,9},{11,10},{12... | collective-permute-start | bytes 196616 | tf_op jit(solution)/shard_map/ppermute | solution.py:29
  44.3 7.3 %collective-permute-start.3 = (f32[2,4,4,2,256]{4,3,2,1,0:T(2,128)S(1)}, f32[2,4,4,2,256]{4,3,2,1,0:T(2,128)S(1)}, u32[]{:S(2)}, u32[]{:S(2)}) collective-permute-start(f32[2,4,4,2,256]{4,3,2,1,0:T(2,128)S(1)} %get-tuple-element.76), channel_id=1, source_target_pairs={{0,1},{1,2},{2,3},{3,4},{4,5},{5,6},{6,7},{8,9},{9,10},{10,11},{11... | collective-permute-start | bytes 196616 | tf_op jit(solution)/shard_map/ppermute | solution.py:27
  81.0 7.7 %collective-permute-start.4 = (f32[2,4,4,2,256]{4,3,2,1,0:T(2,128)S(1)}, f32[2,4,4,2,256]{4,3,2,1,0:T(2,128)S(1)}, u32[]{:S(2)}, u32[]{:S(2)}) collective-permute-start(f32[2,4,4,2,256]{4,3,2,1,0:T(2,128)S(1)} %get-tuple-element.50), channel_id=1, source_target_pairs={{1,0},{2,1},{3,2},{4,3},{5,4},{6,5},{7,6},{9,8},{10,9},{11,10},{12... | collective-permute-start | bytes 196616 | tf_op jit(solution)/shard_map/ppermute | solution.py:29
  82.3 8.2 %collective-permute-start.5 = (f32[2,4,4,2,256]{4,3,2,1,0:T(2,128)S(1)}, f32[2,4,4,2,256]{4,3,2,1,0:T(2,128)S(1)}, u32[]{:S(2)}, u32[]{:S(2)}) collective-permute-start(f32[2,4,4,2,256]{4,3,2,1,0:T(2,128)S(1)} %get-tuple-element.51), channel_id=1, source_target_pairs={{0,1},{1,2},{2,3},{3,4},{4,5},{5,6},{6,7},{8,9},{9,10},{10,11},{11... | collective-permute-start | bytes 196616 | tf_op jit(solution)/shard_map/ppermute | solution.py:27
  88.6 1.8 %copy-start.1 = (f32[2,4,4,2,256]{4,3,2,1,0:T(2,128)}, f32[2,4,4,2,256]{4,3,2,1,0:T(2,128)S(1)}, u32[]{:S(2)}) copy-start(f32[2,4,4,2,256]{4,3,2,1,0:T(2,128)S(1)} %collective-permute-done.4) | copy-start | bytes 196612
  90.4 0.6 copy-start.2
  104.3 7.4 %collective-permute-start.6 = (f32[2,4,4,2,256]{4,3,2,1,0:T(2,128)S(1)}, f32[2,4,4,2,256]{4,3,2,1,0:T(2,128)S(1)}, u32[]{:S(2)}, u32[]{:S(2)}) collective-permute-start(f32[2,4,4,2,256]{4,3,2,1,0:T(2,128)S(1)} %get-tuple-element.31), channel_id=1, source_target_pairs={{1,0},{2,1},{3,2},{4,3},{5,4},{6,5},{7,6},{9,8},{10,9},{11,10},{12... | collective-permute-start | bytes 196616 | tf_op jit(solution)/shard_map/ppermute | solution.py:29
  105.6 7.2 %collective-permute-start.7 = (f32[2,4,4,2,256]{4,3,2,1,0:T(2,128)S(1)}, f32[2,4,4,2,256]{4,3,2,1,0:T(2,128)S(1)}, u32[]{:S(2)}, u32[]{:S(2)}) collective-permute-start(f32[2,4,4,2,256]{4,3,2,1,0:T(2,128)S(1)} %get-tuple-element.32), channel_id=1, source_target_pairs={{0,1},{1,2},{2,3},{3,4},{4,5},{5,6},{6,7},{8,9},{9,10},{10,11},{11... | collective-permute-start | bytes 196616 | tf_op jit(solution)/shard_map/ppermute | solution.py:27
where the time goes:
time: 147 us; the launch traced here: 146 us
  other arithmetic  46.4 us (32%)
  local copies, waits for them, and re-layouts  35.6 us (24%)
  blocking collectives  32.5 us (22%)
  starting transfers between devices  26.7 us (18%)
  waiting for transfers between devices  3.75 us (3%)
    add x4, other arithmetic, advance_core(): updated = centre + TIME_STEP * (tendency + forcing)  27 us
    psum x1, blocking collectives, body(): total = lax.psum(partial_total, 'tile')  24.4 us
    ppermute x4, starting transfers between devices, extended(): lax.ppermute(tail, axis, [(i, (i + 1) % count) for i in range(ends)])  21.6 us
    slice x8, local copies, waits for them, and re-layouts, advance_core(): west_two = jnp.roll(centre, 2, axis=4)  10.6 us
    slice x8, local copies, waits for them, and re-layouts, advance_core(): east_one = jnp.roll(centre, -1, axis=4)  10.5 us
    all_to_all x1, blocking collectives, body(): lax.all_to_all(outgoing, 'member', split_axis=0, concat_axis=0, tiled=True)  8.18 us
    mul x4, other arithmetic, advance_core(): east_wind * slope_x + north_wind * slope_y  7.68 us
    slice x8, local copies, waits for them, and re-layouts, advance_core(): lower = jnp.concatenate([centre[:, :, :1], centre[:, :, :-1]], axis=2)  7.26 us
  transfers between devices with their start and end apart: 8, of which 3 were waited for; matrix products, arithmetic and copies ran while one was open for 14% of the time, Pallas kernels for 0%

commit v1 on v0

v1 whole, which is shorter than its diff:
```python
import functools

import jax
import jax.numpy as jnp
from jax import lax
from jax.experimental import pallas as pl
from jax.experimental.pallas import tpu as pltpu
from jax.sharding import PartitionSpec as P

TIME_STEP = 0.15
DIFFUSION = 0.2
MIXING = 0.1
CORIOLIS = 0.5
BUOYANCY_GAIN = 0.3
STRATIFICATION = 0.3
SATURATION = 0.5
LATENT = 0.5

HALO = 8
PERT_HALO = 8
MESH = pl.DeviceIdType.MESH


def exchange_kernel(tiles, state, pert, other, etop, ebot, ptop, pbot, ssem, rsem):
    t = lax.axis_index("tile")
    m = lax.axis_index("member")
    has_lo = t > 0
    has_hi = t < tiles - 1
    rows = state.shape[3]
    barrier = pltpu.get_barrier_semaphore()
    partner = {"member": 1 - m}
    below = {"tile": t - 1}
    above = {"tile": t + 1}

    pl.semaphore_signal(barrier, inc=1, device_id=partner, device_id_type=MESH)

    @pl.when(has_lo)
    def _():
        pl.semaphore_signal(barrier, inc=1, device_id=below, device_id_type=MESH)

    @pl.when(has_hi)
    def _():
        pl.semaphore_signal(barrier, inc=1, device_id=above, device_id_type=MESH)

    pl.semaphore_wait(barrier, 1 + has_lo.astype(jnp.int32) + has_hi.astype(jnp.int32))

    def remote(src, dst, number, where):
        return pltpu.make_async_remote_copy(
            src_ref=src, dst_ref=dst, send_sem=ssem.at[number], recv_sem=rsem.at[number],
            device_id=where, device_id_type=MESH,
        )

    head = pl.ds(0, HALO)
    tail = pl.ds(rows - HALO, HALO)
    phead = pl.ds(0, PERT_HALO)
    ptail = pl.ds(rows - PERT_HALO, PERT_HALO)
    main = remote(state, other, 0, partner)
    down = remote(state.at[:, :, :, head, :], ebot.at[0], 1, below)
    up = remote(state.at[:, :, :, tail, :], etop.at[0], 2, above)
    pdown = remote(pert.at[:, :, :, phead, :], pbot, 3, below)
    pup = remote(pert.at[:, :, :, ptail, :], ptop, 4, above)
    fbot = remote(ebot.at[0], ebot.at[1], 5, partner)
    ftop = remote(etop.at[0], etop.at[1], 6, partner)

    @pl.when(has_lo)
    def _():
        down.start()

    @pl.when(has_hi)
    def _():
        up.start()

    @pl.when(has_lo)
    def _():
        pdown.start()

    @pl.when(has_hi)
    def _():
        pup.start()

    main.start()

    @pl.when(has_hi)
    def _():
        down.wait_recv()
        fbot.start()

    @pl.when(has_lo)
    def _():
        up.wait_recv()
        ftop.start()

    @pl.when(has_hi)
    def _():
        up.wait_send()
        pup.wait_send()
        pdown.wait_recv()
        fbot.wait()

    @pl.when(has_lo)
    def _():
        down.wait_send()
        pdown.wait_send()
        pup.wait_recv()
        ftop.wait()

    main.wait()


def exchange(state, pert):
    tiles = lax.axis_size("tile")
    lead = state.shape[:3]
    columns = state.shape[4]
    edge = jax.ShapeDtypeStruct((2,) + lead + (HALO, columns), state.dtype)
    pedge = jax.ShapeDtypeStruct(lead + (PERT_HALO, columns), state.dtype)
    anywhere = pl.BlockSpec(memory_space=pl.ANY)
    return pl.pallas_call(
        functools.partial(exchange_kernel, tiles),
        out_shape=[jax.ShapeDtypeStruct(state.shape, state.dtype), edge, edge, pedge, pedge],
        in_specs=[anywhere] * 2,
        out_specs=[anywhere] * 5,
        scratch_shapes=[pltpu.SemaphoreType.DMA((7,)), pltpu.SemaphoreType.DMA((7,))],
        compiler_params=pltpu.CompilerParams(collective_id=0, has_side_effects=True),
        name="exchange",
    )(state, pert)


def advance_block(src, start, columns, emit):
    window = src.at[:, :, pl.ds(pl.multiple_of(start - 8, 8), 24), :]

    def at(field, level, shift):
        return window[field, level, pl.ds(8 + shift, 8), :]

    levels = src.shape[1]
    for level in range(levels):
        centre = [at(field, level, 0) for field in range(4)]
        east, north, buoyancy, _ = centre
        east_scaled = east * (TIME_STEP / 12.0)
        north_scaled = north * (TIME_STEP / 12.0)
        updated = []
        for field in range(4):
            c = centre[field]
            n1 = at(field, level, 1)
            s1 = at(field, level, -1)
            n2 = at(field, level, 2)
            s2 = at(field, level, -2)
            e1 = pltpu.roll(c, columns - 1, 1)
            w1 = pltpu.roll(c, 1, 1)
            e2 = pltpu.roll(c, columns - 2, 1)
            w2 = pltpu.roll(c, 2, 1)
            upper = at(field, level + 1, 0) if level + 1 < levels else c
            lower = at(field, level - 1, 0) if level > 0 else c
            slope_x = 8.0 * (e1 - w1) - (e2 - w2)
            slope_y = 8.0 * (n1 - s1) - (n2 - s2)
            new = c * (1.0 - TIME_STEP * (4.0 * DIFFUSION + 2.0 * MIXING))
            new = new + (TIME_STEP * DIFFUSION) * ((n1 + s1) + (e1 + w1))
            new = new + (TIME_STEP * MIXING) * (upper + lower)
            new = new - (east_scaled * slope_x + north_scaled * slope_y)
            if field == 0:
                new = new + (TIME_STEP * CORIOLIS) * north
            elif field == 1:
                new = new + ((TIME_STEP * BUOYANCY_GAIN) * buoyancy - (TIME_STEP * CORIOLIS) * east)
            elif field == 2:
                new = new - (TIME_STEP * STRATIFICATION) * north
            updated.append(new)
        excess = jnp.maximum(updated[3] - SATURATION * jnp.exp(0.1 * updated[2]), 0.0)
        updated[2] = updated[2] + LATENT * excess
        updated[3] = updated[3] - excess
        for field in range(4):
            emit(field, level, updated[field])


def compute_kernel(total_rows, ancestors, state, other, etop, ebot, pert, ptop, pbot,
                   out, total, a, b, p, o, sems, osem):
    slots, rows, columns = state.shape[0], state.shape[3], state.shape[4]
    t = lax.axis_index("tile")
    owner = lax.axis_index("member")
    has_lo = t > 0
    has_hi = t < lax.axis_size("tile") - 1
    row0 = t * rows
    sources = [ancestors[owner * slots + s] for s in range(slots)]
    holders = [lax.div(source, slots) for source in sources]
    places = [lax.rem(source, slots) for source in sources]
    base = 8 + HALO
    blocks = rows // 8

    def copies(s, where, index):
        source = other if where else state
        return [
            (None, pltpu.make_async_copy(source.at[index], a.at[s, :, :, pl.ds(base, rows), :], sems.at[s, 0])),
            (None, pltpu.make_async_copy(pert.at[s], p.at[s, :, :, pl.ds(base, rows), :], sems.at[s, 1])),
            (has_lo, pltpu.make_async_copy(etop.at[where, index], a.at[s, :, :, pl.ds(8, 8), :], sems.at[s, 2])),
            (has_lo, pltpu.make_async_copy(ptop.at[s], p.at[s, :, :, pl.ds(8, 8), :], sems.at[s, 3])),
            (has_hi, pltpu.make_async_copy(ebot.at[where, index], a.at[s, :, :, pl.ds(base + rows, 8), :], sems.at[s, 4])),
            (has_hi, pltpu.make_async_copy(pbot.at[s], p.at[s, :, :, pl.ds(base + rows, 8), :], sems.at[s, 5])),
        ]

    def start_all(s, where):
        for condition, copy in copies(s, where, places[s]):
            if condition is None:
                copy.start()
            else:
                pl.when(condition)(copy.start)

    for s in range(slots):
        pl.when(holders[s] == owner)(functools.partial(start_all, s, 0))
        pl.when(holders[s] != owner)(functools.partial(start_all, s, 1))

    def clear(ref):
        zero = jnp.zeros(ref.shape[:2] + (8, columns), jnp.float32)

        @pl.when(jnp.logical_not(has_lo))
        def _():
            ref[:, :, pl.ds(8, 8), :] = zero

        @pl.when(jnp.logical_not(has_hi))
        def _():
            ref[:, :, pl.ds(base + rows, 8), :] = zero

    def run_slot(s, carry):
        for condition, copy in copies(s, 0, 0):
            if condition is None:
                copy.wait()
            else:
                pl.when(condition)(copy.wait)
        first, second, bumps, result = a.at[s], b, p.at[s], o.at[s]
        clear(first)

        def plain(src, dst, add):
            def block(i, none):
                start = pl.multiple_of(i * 8, 8)

                def emit(field, level, value):
                    if add is not None:
                        value = value + add[field, level, pl.ds(start, 8), :]
                    dst[field, level, pl.ds(start, 8), :] = value

                advance_block(src, start, columns, emit)
                return none

            lax.fori_loop(1, blocks + 3, block, 0)
            clear(dst)

        plain(first, second, None)
        plain(second, first, bumps)
        plain(first, second, None)

        def last(i, sums):
            start = pl.multiple_of(i * 8, 8)
            there = pl.multiple_of(i * 8 - base, 8)
            row = lax.broadcasted_iota(jnp.int32, (8, columns), 0) + (row0 + there)
            weight = 1.0 + 2.0 * row.astype(jnp.float32) / (total_rows - 1)
            squares = []

            def emit(field, level, value):
                if field == 2:
                    squares.append(value * value)
                result[field, level, pl.ds(there, 8), :] = value

            advance_block(second, start, columns, emit)
            return sums + weight * functools.reduce(jnp.add, squares)

        total[s] = lax.fori_loop(2, blocks + 2, last, jnp.zeros((8, columns), jnp.float32))
        pltpu.make_async_copy(result, out.at[s], osem.at[s]).start()
        return carry

    lax.fori_loop(0, slots, run_slot, 0)
    for s in range(slots):
        pltpu.make_async_copy(o.at[s], out.at[s], osem.at[s]).wait()


def compute(ancestors, state, other, etop, ebot, pert, ptop, pbot, total_rows):
    slots, fields, levels, rows, columns = state.shape
    anywhere = pl.BlockSpec(memory_space=pl.ANY)
    tall = rows + 2 * HALO + 16
    return pl.pallas_call(
        functools.partial(compute_kernel, total_rows),
        out_shape=[
            jax.ShapeDtypeStruct(state.shape, state.dtype),
            jax.ShapeDtypeStruct((slots, 8, columns), jnp.float32),
        ],
        in_specs=[pl.BlockSpec(memory_space=pltpu.SMEM)] + [anywhere] * 7,
        out_specs=[anywhere, pl.BlockSpec(memory_space=pltpu.VMEM)],
        scratch_shapes=[
            pltpu.VMEM((slots, fields, levels, tall, columns), jnp.float32),
            pltpu.VMEM((fields, levels, tall, columns), jnp.float32),
            pltpu.VMEM((slots, fields, levels, tall, columns), jnp.float32),
            pltpu.VMEM((slots, fields, levels, rows, columns), jnp.float32),
            pltpu.SemaphoreType.DMA((slots, 6)),
            pltpu.SemaphoreType.DMA((slots,)),
        ],
        compiler_params=pltpu.CompilerParams(vmem_limit_bytes=61000 * 1024),
        name="advance",
    )(ancestors, state, other, etop, ebot, pert, ptop, pbot)


def reduce_kernel(tiles, partial, total, mine, landed, ssem, rsem):
    t = lax.axis_index("tile")
    barrier = pltpu.get_barrier_semaphore()
    for step in range(1, tiles):
        peer = {"tile": lax.rem(t + step, tiles)}
        pl.semaphore_signal(barrier, inc=1, device_id=peer, device_id_type=MESH)
    summed = jnp.sum(jnp.sum(partial[...], axis=2, keepdims=True), axis=1, keepdims=True)
    mine[...] = jnp.broadcast_to(summed, mine.shape)
    pl.semaphore_wait(barrier, tiles - 1)
    copies = []
    for step in range(1, tiles):
        copies.append(pltpu.make_async_remote_copy(
            src_ref=mine, dst_ref=landed.at[step - 1],
            send_sem=ssem.at[step - 1], recv_sem=rsem.at[step - 1],
            device_id={"tile": lax.rem(t + step, tiles)}, device_id_type=MESH,
        ))
    for copy in copies:
        copy.start()
    for copy in copies:
        copy.wait()
    sums = mine[...]
    for step in range(1, tiles):
        sums = sums + landed[step - 1]
    total[...] = sums


def reduce_tiles(partial):
    tiles = lax.axis_size("tile")
    shape = (partial.shape[0], 8, 128)
    inside = pl.BlockSpec(memory_space=pltpu.VMEM)
    return pl.pallas_call(
        functools.partial(reduce_kernel, tiles),
        out_shape=jax.ShapeDtypeStruct(shape, jnp.float32),
        in_specs=[inside],
        out_specs=inside,
        scratch_shapes=[
            pltpu.VMEM(shape, jnp.float32),
            pltpu.VMEM((tiles - 1,) + shape, jnp.float32),
            pltpu.SemaphoreType.DMA((tiles - 1,)),
            pltpu.SemaphoreType.DMA((tiles - 1,)),
        ],
        compiler_params=pltpu.CompilerParams(collective_id=1, has_side_effects=True),
        name="reduce_tiles",
    )(partial)


def body(state, pert, ancestors):
    slots, fields, levels, rows, columns = state.shape
    tiles = lax.axis_size("tile")
    total_rows = rows * tiles
    other, etop, ebot, ptop, pbot = exchange(state, pert)
    evolved, partial = compute(ancestors, state, other, etop, ebot, pert, ptop, pbot, total_rows)
    total = reduce_tiles(partial)[:, 0, 0]
    return evolved, total / (levels * total_rows * columns)


def solution(mesh):
    spec = P(("groups", "member"), None, None, "tile", None)
    return jax.shard_map(
        body,
        mesh=mesh,
        in_specs=(spec, spec, P("groups")),
        out_specs=(spec, P(("groups", "member"))),
        check_vma=False,
    )
```

time: 147 us -> 61.6 us (0.42)
  Pallas kernels: 0 us -> 59.4 us
  other arithmetic: 46.4 us -> 1.31 us
  local copies, waits for them, and re-layouts: 35.6 us -> 0 us
  blocking collectives: 32.5 us -> 0 us
  starting transfers between devices: 26.7 us -> 0 us
  waiting for transfers between devices: 3.75 us -> 0 us
    pallas_call x0 -> x3, Pallas kernels: none -> 59.4 us  [the longest x1 25.9 us: exchange(): pl.pallas_call(functools.partial(exchange_kernel, tiles), out_shape=[jax....]
    slice x32 -> x0, local copies, waits for them, and re-layouts: 29.9 us -> none  [the longest x8 10.6 us: advance_core(): west_two = jnp.roll(centre, 2, axis=4)]
    add x7 -> x0, other arithmetic: 29.1 us -> none  [the longest x4 27 us: advance_core(): updated = centre + TIME_STEP * (tendency + forcing)]
    ppermute x8 -> x0, starting transfers between devices: 26.7 us -> none  [the longest x4 21.6 us: extended(): lax.ppermute(tail, axis, [(i, (i + 1) % count) for i in range(ends)])]
    psum x1 -> x0, blocking collectives: 24.4 us -> none  [body(): total = lax.psum(partial_total, 'tile')]
    all_to_all x1 -> x0, blocking collectives: 8.18 us -> none  [body(): lax.all_to_all(outgoing, 'member', split_axis=0, concat_axis=0, tiled=True)]
    mul x4 -> x0, other arithmetic: 7.68 us -> none  [advance_core(): east_wind * slope_x + north_wind * slope_y]
    ppermute x8 -> x0, waiting for transfers between devices: 3.75 us -> none  [the longest x4 3.74 us: extended(): lax.ppermute(tail, axis, [(i, (i + 1) % count) for i in range(ends)])]
  transfers between devices with their start and end apart: 8 -> 0, of which waited for: 3 -> 0; matrix products, arithmetic and copies ran while one was open for 14% -> 0% of each run, Pallas kernels for 0% -> 0%
where the time goes in v1:
time: 61.6 us; the launch traced here: 61.3 us
  Pallas kernels  59.4 us (96%)
  other arithmetic  1.31 us (2%)
  between operations  0.65 us (1%)
    pallas_call x1, Pallas kernels, exchange(): pl.pallas_call(functools.partial(exchange_kernel, tiles), out_shape=[jax....  25.9 us
    pallas_call x1, Pallas kernels, compute(): pl.pallas_call(functools.partial(compute_kernel, total_rows), out_shape=[...  23.5 us
    pallas_call x1, Pallas kernels, reduce_tiles(): pl.pallas_call(functools.partial(reduce_kernel, tiles), out_shape=jax.Sha...  9.96 us
    div x1, other arithmetic, body(): return (evolved, total / (levels * total_rows * columns))  1.31 us

profile of v1, /device:TPU:0, one launch (start us, length us, event | category | flops | bytes accessed | tf_op | source)
XLA Modules:
  0.0 61.3 jit_solution(1923785362594521744)
XLA Ops:
  0.6 25.9 %exchange.1 = (f32[2,4,4,64,256]{4,3,2,1,0:T(8,128)}, f32[2,2,4,4,8,256]{5,4,3,2,1,0:T(8,128)}, f32[2,2,4,4,8,256]{5,4,3,2,1,0:T(8,128)}, f32[2,4,4,8,256]{4,3,2,1,0:T(8,128)}, f32[2,4,4,8,256]{4,3,2,1,0:T(8,128)}) custom-call(f32[2,4,4,64,256]{4,3,2,1,0:T(8,128)} %state.3, f32[2,4,4,64,256]{4,3,2,1,0:T(8,128)} %pert.3), custom_call_target="tpu_custom_call" | custom-call | tf_op jit(solution)/shard_map/exchange/pallas_call | solution.py:117
  26.5 23.5 %advance.1 = (f32[2,4,4,64,256]{4,3,2,1,0:T(8,128)}, f32[2,8,256]{2,1,0:T(8,128)}) custom-call(s32[4]{0:T(128)} %ancestors.1, f32[2,4,4,64,256]{4,3,2,1,0:T(8,128)} %state.3, f32[2,4,4,64,256]{4,3,2,1,0:T(8,128)} %get-tuple-element.9.other, f32[2,2,4,4,8,256]{5,4,3,2,1,0:T(8,128)} %get-tuple-element.10.etop, ...), custom_call_target="tpu_custom_call" | custom-call | tf_op jit(solution)/shard_map/advance/pallas_call | solution.py:276
  50.0 10.0 %reduce_tiles.1 = f32[2,8,128]{2,1,0:T(8,128)} custom-call(f32[2,8,256]{2,1,0:T(8,128)} %get-tuple-element.15.partial), custom_call_target="tpu_custom_call" | custom-call | tf_op jit(solution)/shard_map/reduce_tiles/pallas_call | solution.py:327
  60.0 1.3 %multiply_reduce_fusion = f32[2]{0:T(128)} fusion(f32[2,8,128]{2,1,0:T(8,128)} %reduce_tiles.1), kind=kLoop, calls=%fused_computation | loop fusion | flops 2 | bytes 16 | tf_op jit(solution)/shard_map/div | solution.py:350
